TPU v7x, 32 devices: a whole 2x2x4 slice. The times are simulated.
32 devices in a mesh: date: 2 (over y), trade: 8 (over z, x), path: 2 (over core).
Axes of the slice: x: 2, y: 2, z: 4, core: 2. Of those that a mesh axis runs over, the one named last changes fastest.
Arguments:
- basis_values: bfloat16 [2048, 512], P(('date', 'path')), parts along dimension 0, may hold values from -6 to 6
- coefficients: bfloat16 [2560, 512], P(('date', 'trade')), parts along dimension 0, may hold values from -0.25 to 0.25
- trade_cpty: int32 [1280], P('trade'), may hold values from 0 to 127, as said below
- trade_bucket: int32 [1280], P('trade'), may hold values from 0 to 127
- risk_weights: float32 [128], replicated, may hold values from 0.5 to 2
- correlation: float32 [128, 128], replicated, may hold values from 0 to 1, as said below
- funding_spread: float32 [128], P('trade'), may hold values from 0.5 to 2
Outputs:
- margin: float32 [128, 2048], P('trade', ('date', 'path')), parts along dimension 1
- basis_adjoint: bfloat16 [2048, 512], P(('date', 'path')), parts along dimension 0
There are 2 independent parts, one for each index of `date`. A program takes and returns all parts, laid end to end along the dimension named above; an argument that names none is the same for every part. Nothing has to cross between parts.
Inputs may be any that keep to these rules, and one draw needn't show every extreme that they name: `trade_cpty`: counterparty c belongs to owner block c // 16. Among the trades of one device, at most 40 belong to counterparties of one owner block; in every draw one owner block receives exactly 40 from every device. Counterparties differ in size. `correlation`: symmetric positive definite with unit diagonal; smallest eigenvalue at least 0.01; entries positive.
All inputs are finite; a program needn't handle non-finite values.
Results may differ from a plain program's by a relative error of at most 0.0034.
Values may be sent and summed in bfloat16 or wider, within the bound.
No kernel may reach another device: no remote copies, remote signals or barrier semaphores. Data moves between devices by JAX's collectives and lax.ppermute only.
A program may use at most 64 MiB of HBM per device.

v0:
```python
import jax
import jax.numpy as jnp
from jax import lax
from jax.sharding import PartitionSpec as P


def margin_terms(arrived, got_codes, risk_weights, correlation, funding_spread):
    path_rows = arrived.shape[0]
    cpty_count = funding_spread.shape[0]
    bucket_count = risk_weights.shape[0]
    is_filled = got_codes >= 0
    column_ids = jnp.arange(cpty_count * bucket_count, dtype=jnp.int32)
    hot_table = (got_codes[:, None] == column_ids[None, :]).astype(jnp.bfloat16)
    bucket_sums = jnp.dot(arrived, hot_table, preferred_element_type=jnp.float32)
    weighted = (
        bucket_sums.reshape(path_rows, cpty_count, bucket_count) * risk_weights[None, None, :]
    )
    rho_w = jnp.einsum("pcb,db->pcd", weighted, correlation, precision=lax.Precision.HIGHEST)
    margin_now = jnp.sqrt(jnp.sum(weighted * rho_w, axis=2) + 1e-06)
    sens_bar = (
        funding_spread[None, :, None] * risk_weights[None, None, :] * rho_w / margin_now[:, :, None]
    )
    flat_bar = sens_bar.reshape(path_rows, cpty_count * bucket_count)
    safe_codes = jnp.where(is_filled, got_codes, 0)
    slot_bar = jnp.take(flat_bar, safe_codes, axis=1) * is_filled[None, :].astype(jnp.float32)
    return (margin_now, slot_bar.astype(jnp.bfloat16))


def body(
    basis_values, coefficients, trade_cpty, trade_bucket, risk_weights, correlation, funding_spread
):
    owners = lax.axis_size("trade")
    per_device = coefficients.shape[0]
    capacity = max(2, 2 * per_device // owners)
    slot_total = owners * capacity
    cpty_count = funding_spread.shape[0]
    bucket_count = risk_weights.shape[0]
    path_rows = basis_values.shape[0]
    owner_of = trade_cpty // cpty_count
    trade_code = trade_cpty % cpty_count * bucket_count + trade_bucket
    position = jnp.arange(per_device, dtype=jnp.int32)
    same_owner = owner_of[:, None] == owner_of[None, :]
    earlier = position[None, :] < position[:, None]
    rank_in = jnp.sum((same_owner & earlier).astype(jnp.int32), axis=1)
    slot_index = owner_of * capacity + rank_in
    codes_out = jnp.full((slot_total,), -1, jnp.int32).at[slot_index].set(trade_code)
    got_codes = lax.all_to_all(codes_out, "trade", split_axis=0, concat_axis=0, tiled=True)
    delta_rows = lax.dot_general(
        basis_values, coefficients, (((1,), (1,)), ((), ())), preferred_element_type=jnp.float32
    ).astype(jnp.bfloat16)
    outgoing = jnp.zeros((path_rows, slot_total), jnp.bfloat16).at[:, slot_index].set(delta_rows)
    arrived = lax.all_to_all(outgoing, "trade", split_axis=1, concat_axis=1, tiled=True)
    margin_now, slot_bar = margin_terms(
        arrived, got_codes, risk_weights, correlation, funding_spread
    )
    returned = lax.all_to_all(slot_bar, "trade", split_axis=1, concat_axis=1, tiled=True)
    delta_bar = returned[:, slot_index]
    partial_adj = jnp.dot(delta_bar, coefficients, preferred_element_type=jnp.float32)
    basis_adjoint = lax.psum(partial_adj, "trade").astype(jnp.bfloat16)
    return (margin_now.T, basis_adjoint)


def solution(mesh):
    placed = (
        P(("date", "path"), None),
        P(("date", "trade"), None),
        P("trade"),
        P("trade"),
        P(),
        P(),
        P("trade"),
    )
    return jax.shard_map(
        body,
        mesh=mesh,
        in_specs=placed,
        out_specs=(P("trade", ("date", "path")), P(("date", "path"), None)),
        check_vma=False,
    )
```

profile of v0, /device:TPU:0, one launch (start us, length us, event | category | flops | bytes accessed | tf_op | source)
XLA Modules:
  0.0 130.3 jit_solution(14144373721821639996)
XLA Ops:
  0.6 0.8 fusion.14
  1.4 0.2 convert_reduce_fusion
  1.6 1.1 scatter_custom_fusion.1
  2.7 0.7 all_to_all.25
  3.4 7.3 %all-to-all-start.1 = ((s32[8,40,1]{1,2,0:T(1,128)}), s32[8,40,1]{1,2,0:T(1,128)S(1)}, u32[]{:S(2)}, u32[]{:S(2)}) async-start(s32[8,40,1]{1,2,0:T(1,128)} %all_to_all.25), calls=%async_computation.1 | async-start | bytes 8192 | tf_op jit(solution)/shard_map/all_to_all | solution.py:47
  10.7 1.2 fusion.7
  11.9 1.9 %scatter_custom_fusion = bf16[512,320]{0,1:T(8,128)(2,1)} fusion(s32[160]{0:T(256)S(1)} %compare_select_fusion.4, bf16[160,512]{1,0:T(8,128)(2,1)S(1)} %fusion.7, bf16[]{:T(256)} %constant.45.clone.1), kind=kCustom, calls=%fused_computation.18 | custom fusion | bytes 327682 | tf_op jit(solution)/shard_map/scatter | solution.py:51
  13.8 3.2 %all-to-all-done.1 = s32[8,40,1]{1,2,0:T(1,128)S(1)} async-done(((s32[8,40,1]{1,2,0:T(1,128)}), s32[8,40,1]{1,2,0:T(1,128)S(1)}, u32[]{:S(2)}, u32[]{:S(2)}) %all-to-all-start.1) | async-done | bytes 1312 | tf_op jit(solution)/shard_map/all_to_all | solution.py:47
  17.0 3.4 %all-to-all-start = ((bf16[512,8,40]{0,2,1:T(8,128)(2,1)}), bf16[512,8,40]{0,2,1:T(8,128)(2,1)S(1)}, u32[]{:S(2)}, u32[]{:S(2)}) async-start(bf16[512,8,40]{0,2,1:T(8,128)(2,1)} %bitcast.1), calls=%async_computation | async-start | bytes 655360 | tf_op jit(solution)/shard_map/all_to_all | solution.py:52
  20.5 0.7 broadcast_multiply_fusion
  21.2 0.5 broadcast.164
  21.7 0.7 reduce.7
  22.6 6.9 %all-to-all-done = bf16[512,8,40]{0,2,1:T(8,128)(2,1)S(1)} async-done(((bf16[512,8,40]{0,2,1:T(8,128)(2,1)}), bf16[512,8,40]{0,2,1:T(8,128)(2,1)S(1)}, u32[]{:S(2)}, u32[]{:S(2)}) %all-to-all-start) | async-done | bytes 327712 | tf_op jit(solution)/shard_map/all_to_all | solution.py:52
  29.6 1.4 %fusion.2 = f32[512,16,128]{0,2,1:T(8,128)S(1)} fusion(bf16[512,320,1]{0,1,2:T(8,128)(2,1)S(1)} %bitcast.29, s32[16,128]{1,0:T(8,128)S(1)} %multiply_add_fusion, s32[320]{0:T(512)S(1)} %eq.51), kind=kOutput, calls=%fused_computation.8 | convolution fusion | flops 671744000 | bytes 4531456 | tf_op jit(solution)/shard_map/dot_general | solution.py:14
  31.0 5.5 %multiply_reduce_fusion = (f32[512,16]{0,1:T(8,128)S(1)}, f32[512,16,128]{0,2,1:T(8,128)S(1)}) fusion(f32[512,16,128]{0,2,1:T(8,128)S(1)} %fusion.2, f32[128]{0:T(128)S(1)} %copy-done.3, f32[128,128]{1,0:T(8,128)S(1)} %copy-done.2), kind=kOutput, calls=%fused_computation.5 | convolution fusion | flops 1614798848 | bytes 8487424 | tf_op jit(solution)/shard_map/pcb,db->pcd/dot_general | solution.py:18
  36.4 0.6 add_sqrt_fusion
  37.1 2.4 %multiply_divide_fusion = f32[512,16,128]{0,2,1:T(8,128)} fusion(f32[512,16,128]{0,2,1:T(8,128)S(1)} %get-tuple-element.9, f32[512,16]{0,1:T(8,128)S(1)} %get-tuple-element.2, f32[16,128]{1,0:T(8,128)S(1)} %broadcast_multiply_fusion), kind=kLoop, calls=%fused_computation.4 | loop fusion | flops 2097152 | bytes 8429568 | tf_op jit(solution)/shard_map/div | solution.py:21
  39.5 4.3 %gather_fusion = f32[320,512]{1,0:T(8,128)S(1)} fusion(f32[512,2048]{0,1:T(8,128)} %bitcast.26, s32[1024]{0:T(1024)S(1)} %pad_clamp_fusion.1), kind=kCustom, calls=%fused_computation | custom fusion | bytes 1312000 | tf_op jit(solution)/shard_map/jit(_take)/gather | solution.py:25
  43.8 0.9 multiply_convert_fusion
  44.7 3.6 %all-to-all-start.2 = ((bf16[512,8,40]{0,2,1:T(8,128)(2,1)}), bf16[512,8,40]{0,2,1:T(8,128)(2,1)S(1)}, u32[]{:S(2)}, u32[]{:S(2)}) async-start(bf16[512,8,40]{0,2,1:T(8,128)(2,1)} %multiply_convert_fusion), calls=%async_computation.2 | async-start | bytes 655360 | tf_op jit(solution)/shard_map/all_to_all | solution.py:56
  48.3 9.6 %all-to-all-done.2 = bf16[512,8,40]{0,2,1:T(8,128)(2,1)S(1)} async-done(((bf16[512,8,40]{0,2,1:T(8,128)(2,1)}), bf16[512,8,40]{0,2,1:T(8,128)(2,1)S(1)}, u32[]{:S(2)}, u32[]{:S(2)}) %all-to-all-start.2) | async-done | bytes 327712 | tf_op jit(solution)/shard_map/all_to_all | solution.py:56
  57.9 0.9 gather_fusion.1
  58.8 0.3 fusion.18
  59.2 71.2 %all-reduce.1 = bf16[512,512]{1,0:T(8,128)(2,1)} all-reduce(f32[512,512]{1,0:T(8,128)S(1)} %fusion.18), channel_id=1, replica_groups=mesh['date'=2,'trade'=8,'path'=2] {'trade'}, use_global_device_ids=true, to_apply=%region_4.5 | all-reduce | flops 262144 | bytes 1572864 | tf_op jit(solution)/shard_map/psum | solution.py:59
  (16 shorter events, 0.2 us)
Async XLA Ops:
  0.6 10.0 %copy-start = (bf16[512,512]{1,0:T(8,128)(2,1)S(1)}, bf16[512,512]{1,0:T(8,128)(2,1)}, u32[]{:S(2)}) copy-start(bf16[512,512]{1,0:T(8,128)(2,1)} %param.7) | copy-start | bytes 1572868
  3.4 13.6 %all-to-all-start.1 = ((s32[8,40,1]{1,2,0:T(1,128)}), s32[8,40,1]{1,2,0:T(1,128)S(1)}, u32[]{:S(2)}, u32[]{:S(2)}) async-start(s32[8,40,1]{1,2,0:T(1,128)} %all_to_all.25), calls=%async_computation.1 | async-start | bytes 8192 | tf_op jit(solution)/shard_map/all_to_all | solution.py:47
  11.9 19.0 %copy-start.2 = (f32[128,128]{1,0:T(8,128)S(1)}, f32[128,128]{1,0:T(8,128)}, u32[]{:S(2)}) copy-start(f32[128,128]{1,0:T(8,128)} %param.12) | copy-start | bytes 196612
  11.9 19.0 %copy-start.3 = (f32[128]{0:T(128)S(1)}, f32[128]{0:T(128)}, u32[]{:S(2)}) copy-start(f32[128]{0:T(128)} %param.11) | copy-start | bytes 1540
  17.0 12.5 %all-to-all-start = ((bf16[512,8,40]{0,2,1:T(8,128)(2,1)}), bf16[512,8,40]{0,2,1:T(8,128)(2,1)S(1)}, u32[]{:S(2)}, u32[]{:S(2)}) async-start(bf16[512,8,40]{0,2,1:T(8,128)(2,1)} %bitcast.1), calls=%async_computation | async-start | bytes 655360 | tf_op jit(solution)/shard_map/all_to_all | solution.py:52
  39.5 19.3 %copy-start.1 = (bf16[160,512]{1,0:T(8,128)(2,1)S(1)}, bf16[160,512]{1,0:T(8,128)(2,1)}, u32[]{:S(2)}) copy-start(bf16[160,512]{1,0:T(8,128)(2,1)} %param.8) | copy-start | bytes 491524
  44.7 13.2 %all-to-all-start.2 = ((bf16[512,8,40]{0,2,1:T(8,128)(2,1)}), bf16[512,8,40]{0,2,1:T(8,128)(2,1)S(1)}, u32[]{:S(2)}, u32[]{:S(2)}) async-start(bf16[512,8,40]{0,2,1:T(8,128)(2,1)} %multiply_convert_fusion), calls=%async_computation.2 | async-start | bytes 655360 | tf_op jit(solution)/shard_map/all_to_all | solution.py:56
where the time goes:
time: 131 us; the launch traced here: 130 us
  blocking collectives  71.2 us (54%)
  waiting for transfers between devices  19.8 us (15%)
  starting transfers between devices  14.3 us (11%)
  local copies, waits for them, and re-layouts  9.56 us (7%)
  matrix products  8.42 us (6%)
  other arithmetic  6.37 us (5%)
    psum x1, blocking collectives, body(): basis_adjoint = lax.psum(partial_adj, 'trade').astype(jnp.bfloat16)  71.2 us
    all_to_all x1, waiting for transfers between devices, body(): lax.all_to_all(slot_bar, 'trade', split_axis=1, concat_axis=1, tiled=True)  9.6 us
    all_to_all x1, starting transfers between devices, body(): lax.all_to_all(codes_out, 'trade', split_axis=0, concat_axis=0, tiled=True)  7.25 us
    all_to_all x1, waiting for transfers between devices, body(): lax.all_to_all(outgoing, 'trade', split_axis=1, concat_axis=1, tiled=True)  6.93 us
    dot_general x1, matrix products, margin_terms(): jnp.einsum('pcb,db->pcd', weighted, correlation, precision=lax.Precision....  5.47 us
    gather x1, local copies, waits for them, and re-layouts, margin_terms(): jnp.take(flat_bar, safe_codes, axis=1)  4.27 us
    all_to_all x1, starting transfers between devices, body(): lax.all_to_all(slot_bar, 'trade', split_axis=1, concat_axis=1, tiled=True)  3.6 us
    all_to_all x1, starting transfers between devices, body(): lax.all_to_all(outgoing, 'trade', split_axis=1, concat_axis=1, tiled=True)  3.43 us
  transfers between devices with their start and end apart: 3, of which 3 were waited for; matrix products, arithmetic and copies ran while one was open for 4% of the time, Pallas kernels for 0%

commit v1 on v0

--- a/solution.py
+++ b/solution.py
@@ -53,7 +53,12 @@
     margin_now, slot_bar = margin_terms(
         arrived, got_codes, risk_weights, correlation, funding_spread
     )
-    returned = lax.all_to_all(slot_bar, "trade", split_axis=1, concat_axis=1, tiled=True)
+    returned = jnp.concatenate(
+        lax.all_to_all(
+            jnp.stack(jnp.split(slot_bar, lax.axis_size("trade"), axis=1)), "trade", 0, 0
+        ),
+        axis=1,
+    )
     delta_bar = returned[:, slot_index]
     partial_adj = jnp.dot(delta_bar, coefficients, preferred_element_type=jnp.float32)
     basis_adjoint = lax.psum(partial_adj, "trade").astype(jnp.bfloat16)

time: 131 us -> 135 us (1.031)
  local copies, waits for them, and re-layouts: 9.56 us -> 14.5 us
    unnamed x8 -> x15, local copies, waits for them, and re-layouts: 0.03 us -> 4.37 us
where the time goes in v1:
time: 135 us; the launch traced here: 134 us
  blocking collectives  71 us (53%)
  waiting for transfers between devices  19.8 us (15%)
  local copies, waits for them, and re-layouts  14.5 us (11%)
  starting transfers between devices  14.3 us (11%)
  matrix products  8.43 us (6%)
  other arithmetic  5.62 us (4%)
    psum x1, blocking collectives, body(): basis_adjoint = lax.psum(partial_adj, 'trade').astype(jnp.bfloat16)  71 us
    all_to_all x1, waiting for transfers between devices, body(): lax.all_to_all(jnp.stack(jnp.split(slot_bar, lax.axis_size('trade'), axis...  9.6 us
    all_to_all x1, starting transfers between devices, body(): lax.all_to_all(codes_out, 'trade', split_axis=0, concat_axis=0, tiled=True)  7.25 us
    all_to_all x1, waiting for transfers between devices, body(): lax.all_to_all(outgoing, 'trade', split_axis=1, concat_axis=1, tiled=True)  6.93 us
    dot_general x1, matrix products, margin_terms(): jnp.einsum('pcb,db->pcd', weighted, correlation, precision=lax.Precision....  5.48 us
    unnamed x15, local copies, waits for them, and re-layouts  4.37 us
    gather x1, local copies, waits for them, and re-layouts, margin_terms(): jnp.take(flat_bar, safe_codes, axis=1)  4.27 us
    all_to_all x1, starting transfers between devices, body(): lax.all_to_all(jnp.stack(jnp.split(slot_bar, lax.axis_size('trade'), axis...  3.59 us
  transfers between devices with their start and end apart: 3, of which 3 were waited for; matrix products, arithmetic and copies ran while one was open for 4% of the time, Pallas kernels for 0%

profile of v1, /device:TPU:0, one launch (start us, length us, event | category | flops | bytes accessed | tf_op | source)
XLA Modules:
  0.0 134.4 jit_solution(12626211795828763290)
XLA Ops:
  0.6 0.8 fusion.23
  1.6 1.1 scatter_custom_fusion.1
  2.7 0.7 all_to_all.22
  3.4 7.3 %all-to-all-start.1 = ((s32[8,40,1]{1,2,0:T(1,128)}), s32[8,40,1]{1,2,0:T(1,128)S(1)}, u32[]{:S(2)}, u32[]{:S(2)}) async-start(s32[8,40,1]{1,2,0:T(1,128)} %bitcast.4), calls=%async_computation.1 | async-start | bytes 8192 | tf_op jit(solution)/shard_map/all_to_all | solution.py:47
  10.6 1.2 fusion.7
  11.9 1.9 %scatter_custom_fusion = bf16[512,320]{0,1:T(8,128)(2,1)} fusion(s32[160]{0:T(256)S(1)} %compare_select_fusion.3, bf16[160,512]{1,0:T(8,128)(2,1)S(1)} %fusion.7, bf16[]{:T(256)} %constant.45.clone.1), kind=kCustom, calls=%fused_computation.19 | custom fusion | bytes 327682 | tf_op jit(solution)/shard_map/scatter | solution.py:51
  13.8 3.2 %all-to-all-done.1 = s32[8,40,1]{1,2,0:T(1,128)S(1)} async-done(((s32[8,40,1]{1,2,0:T(1,128)}), s32[8,40,1]{1,2,0:T(1,128)S(1)}, u32[]{:S(2)}, u32[]{:S(2)}) %all-to-all-start.1) | async-done | bytes 1312 | tf_op jit(solution)/shard_map/all_to_all | solution.py:47
  17.0 3.4 %all-to-all-start = ((bf16[512,8,40]{0,2,1:T(8,128)(2,1)}), bf16[512,8,40]{0,2,1:T(8,128)(2,1)S(1)}, u32[]{:S(2)}, u32[]{:S(2)}) async-start(bf16[512,8,40]{0,2,1:T(8,128)(2,1)} %bitcast.1), calls=%async_computation | async-start | bytes 655360 | tf_op jit(solution)/shard_map/all_to_all | solution.py:52
  20.5 0.7 broadcast_multiply_fusion
  21.7 0.7 reduce.7
  22.6 6.9 %all-to-all-done = bf16[512,8,40]{0,2,1:T(8,128)(2,1)S(1)} async-done(((bf16[512,8,40]{0,2,1:T(8,128)(2,1)}), bf16[512,8,40]{0,2,1:T(8,128)(2,1)S(1)}, u32[]{:S(2)}, u32[]{:S(2)}) %all-to-all-start) | async-done | bytes 327712 | tf_op jit(solution)/shard_map/all_to_all | solution.py:52
  29.5 1.4 %fusion.2 = f32[512,16,128]{0,2,1:T(8,128)S(1)} fusion(bf16[512,320,1]{0,1,2:T(8,128)(2,1)S(1)} %bitcast.61, s32[16,128]{1,0:T(8,128)S(1)} %multiply_add_fusion, s32[320]{0:T(512)S(1)} %eq.49), kind=kOutput, calls=%fused_computation.8 | convolution fusion | flops 671744000 | bytes 4531456 | tf_op jit(solution)/shard_map/dot_general | solution.py:14
  30.9 5.5 %multiply_reduce_fusion = (f32[512,16]{0,1:T(8,128)S(1)}, f32[512,16,128]{0,2,1:T(8,128)S(1)}) fusion(f32[512,16,128]{0,2,1:T(8,128)S(1)} %fusion.2, f32[128]{0:T(128)S(1)} %copy-done.3, f32[128,128]{1,0:T(8,128)S(1)} %copy-done.2), kind=kOutput, calls=%fused_computation.5 | convolution fusion | flops 1614798848 | bytes 8487424 | tf_op jit(solution)/shard_map/pcb,db->pcd/dot_general | solution.py:18
  36.4 0.6 add_sqrt_fusion
  37.1 2.4 %multiply_divide_fusion = f32[512,16,128]{0,2,1:T(8,128)} fusion(f32[512,16,128]{0,2,1:T(8,128)S(1)} %get-tuple-element.9, f32[512,16]{0,1:T(8,128)S(1)} %get-tuple-element.2, f32[16,128]{1,0:T(8,128)S(1)} %broadcast_multiply_fusion), kind=kLoop, calls=%fused_computation.4 | loop fusion | flops 2097152 | bytes 8429568 | tf_op jit(solution)/shard_map/div | solution.py:21
  39.5 4.3 %gather_fusion = f32[320,512]{1,0:T(8,128)S(1)} fusion(f32[512,2048]{0,1:T(8,128)} %bitcast.59, s32[1024]{0:T(1024)S(1)} %pad_clamp_fusion.1), kind=kCustom, calls=%fused_computation | custom fusion | bytes 1312000 | tf_op jit(solution)/shard_map/jit(_take)/gather | solution.py:25
  43.9 0.6 fusion.20
  44.5 0.6 fusion.19
  45.2 0.6 fusion.18
  45.8 0.6 fusion.17
  48.9 3.6 %all-to-all-start.2 = ((bf16[8,512,40]{1,2,0:T(8,128)(2,1)}), bf16[8,512,40]{1,2,0:T(8,128)(2,1)S(1)}, u32[]{:S(2)}, u32[]{:S(2)}) async-start(bf16[8,512,40]{1,2,0:T(8,128)(2,1)} %fusion.13), calls=%async_computation.2 | async-start | bytes 655360 | tf_op jit(solution)/shard_map/all_to_all | solution.py:57
  52.5 9.6 %all-to-all-done.2 = bf16[8,512,40]{1,2,0:T(8,128)(2,1)S(1)} async-done(((bf16[8,512,40]{1,2,0:T(8,128)(2,1)}), bf16[8,512,40]{1,2,0:T(8,128)(2,1)S(1)}, u32[]{:S(2)}, u32[]{:S(2)}) %all-to-all-start.2) | async-done | bytes 327712 | tf_op jit(solution)/shard_map/all_to_all | solution.py:57
  62.1 0.9 gather_fusion.1
  63.4 71.0 %all-reduce.1 = bf16[512,512]{1,0:T(8,128)(2,1)} all-reduce(f32[512,512]{1,0:T(8,128)S(1)} %fusion.27), channel_id=1, replica_groups=mesh['date'=2,'trade'=8,'path'=2] {'trade'}, use_global_device_ids=true, to_apply=%region_4.5 | all-reduce | flops 262144 | bytes 1572864 | tf_op jit(solution)/shard_map/psum | solution.py:64
  (24 shorter events, 3.9 us)
Async XLA Ops:
  0.6 10.0 %copy-start = (bf16[512,512]{1,0:T(8,128)(2,1)S(1)}, bf16[512,512]{1,0:T(8,128)(2,1)}, u32[]{:S(2)}) copy-start(bf16[512,512]{1,0:T(8,128)(2,1)} %param.7) | copy-start | bytes 1572868
  3.4 13.6 %all-to-all-start.1 = ((s32[8,40,1]{1,2,0:T(1,128)}), s32[8,40,1]{1,2,0:T(1,128)S(1)}, u32[]{:S(2)}, u32[]{:S(2)}) async-start(s32[8,40,1]{1,2,0:T(1,128)} %bitcast.4), calls=%async_computation.1 | async-start | bytes 8192 | tf_op jit(solution)/shard_map/all_to_all | solution.py:47
  11.9 19.0 %copy-start.2 = (f32[128,128]{1,0:T(8,128)S(1)}, f32[128,128]{1,0:T(8,128)}, u32[]{:S(2)}) copy-start(f32[128,128]{1,0:T(8,128)} %param.12) | copy-start | bytes 196612
  11.9 19.0 %copy-start.3 = (f32[128]{0:T(128)S(1)}, f32[128]{0:T(128)}, u32[]{:S(2)}) copy-start(f32[128]{0:T(128)} %param.11) | copy-start | bytes 1540
  17.0 12.5 %all-to-all-start = ((bf16[512,8,40]{0,2,1:T(8,128)(2,1)}), bf16[512,8,40]{0,2,1:T(8,128)(2,1)S(1)}, u32[]{:S(2)}, u32[]{:S(2)}) async-start(bf16[512,8,40]{0,2,1:T(8,128)(2,1)} %bitcast.1), calls=%async_computation | async-start | bytes 655360 | tf_op jit(solution)/shard_map/all_to_all | solution.py:52
  39.5 23.5 %copy-start.1 = (bf16[160,512]{1,0:T(8,128)(2,1)S(1)}, bf16[160,512]{1,0:T(8,128)(2,1)}, u32[]{:S(2)}) copy-start(bf16[160,512]{1,0:T(8,128)(2,1)} %param.8) | copy-start | bytes 491524
  48.9 13.2 %all-to-all-start.2 = ((bf16[8,512,40]{1,2,0:T(8,128)(2,1)}), bf16[8,512,40]{1,2,0:T(8,128)(2,1)S(1)}, u32[]{:S(2)}, u32[]{:S(2)}) async-start(bf16[8,512,40]{1,2,0:T(8,128)(2,1)} %fusion.13), calls=%async_computation.2 | async-start | bytes 655360 | tf_op jit(solution)/shard_map/all_to_all | solution.py:57
